TPU v7x, 256 devices: a whole 4x4x8 slice. The times are simulated.
256 devices in a mesh: bl: 64 (over y, z, core), ch: 4 (over x).
Axes of the slice: x: 4, y: 4, z: 8, core: 2. Of those that a mesh axis runs over, the one named last changes fastest.
Arguments:
- facet_grid: bfloat16 [4, 64, 16, 1024], P(None, None, None, 'ch'), may hold values from -0.75 to 0.75
- kernel: bfloat16 [131072, 1024], P('bl', 'ch'), may hold values from -0.1875 to 0.1875
- tile_of: int32 [256], P('bl'), may hold values from 0 to 3
- observed: bfloat16 [64, 2, 131072], P('ch', None, 'bl'), may hold values from -6 to 6
- flags: int32 [64, 131072], P('ch', 'bl'), may hold values 0 or 1
- pairs: int32 [2, 131072], P(None, 'bl'), may hold values from 0 to 511, as said below
- solver_order: int32 [512], replicated, may hold values from 0 to 511, as said below
Outputs:
- gains: float32 [64, 16, 512], P('ch', None, 'bl')
Inputs may be any that keep to these rules, and one draw needn't show every extreme that they name: `solver_order`: each station appears once. `pairs`: for row r, with j = (r mod 2048) // 32, the first station is solver_order[8 * j + m] for some m below 8; the second station differs from the first.
All inputs are finite; a program needn't handle non-finite values. No bound on the sum of `flags` on one device may be relied on, other than what follows from the above.
Results may differ from a plain program's by a relative error of at most 0.013.
Values may be sent and summed in bfloat16 or wider, within the bound.
No kernel may reach another device: no remote copies, remote signals or barrier semaphores. Data moves between devices by JAX's collectives and lax.ppermute only.
A program may use at most 128 MiB of HBM per device.

v0:
```python
import jax
import jax.numpy as jnp
from jax import lax
from jax.sharding import PartitionSpec as P

S = 512
ND = 8
ITERS = 4


def extended(shard, sides, width):
    for axis, dim in sides:
        devices, length = (lax.axis_size(axis), shard.shape[dim])
        up = [(i, (i + 1) % devices) for i in range(devices - 1)]
        down = [(j, i) for i, j in up]
        last = lax.slice_in_dim(shard, length - width, length, axis=dim)
        initial = lax.slice_in_dim(shard, 0, width, axis=dim)
        before = lax.ppermute(last, axis, up)
        after = lax.ppermute(initial, axis, down)
        shard = jnp.concatenate([before, shard, after], axis=dim)
    return shard


def lookup(gain_flat, pick):
    return jnp.dot(
        gain_flat, pick, precision=lax.Precision.HIGHEST, preferred_element_type=jnp.float32
    )


def row_terms(model_vis, visible, far_gain, near_gain):
    channels = model_vis.shape[0]
    row_count = model_vis.shape[2]
    model_pair = model_vis.reshape(channels, ND, 2, row_count)
    model_re = model_pair[:, :, 0].astype(jnp.float32)
    model_im = model_pair[:, :, 1].astype(jnp.float32)
    far_pair = far_gain.reshape(channels, ND, 2, row_count)
    near_pair = near_gain.reshape(channels, ND, 2, row_count)
    far_re = far_pair[:, :, 0]
    far_im = far_pair[:, :, 1]
    near_re = near_pair[:, :, 0]
    near_im = near_pair[:, :, 1]
    prod_re = model_re * far_re + model_im * far_im
    prod_im = model_im * far_re - model_re * far_im
    pred_re = jnp.sum(near_re * prod_re - near_im * prod_im, axis=1)
    pred_im = jnp.sum(near_re * prod_im + near_im * prod_re, axis=1)
    resid_re = visible[:, 0].astype(jnp.float32) - pred_re
    resid_im = visible[:, 1].astype(jnp.float32) - pred_im
    cross_re = prod_re * resid_re[:, None, :] + prod_im * resid_im[:, None, :]
    cross_im = prod_re * resid_im[:, None, :] - prod_im * resid_re[:, None, :]
    power = prod_re * prod_re + prod_im * prod_im
    stacked = jnp.concatenate([cross_re, cross_im, power], axis=1)
    return stacked.reshape(channels * 3 * ND, row_count)


def update_gains(gain_shard, sum_re, sum_im, power):
    channels = gain_shard.shape[0]
    owned = gain_shard.shape[2]
    gain_pair = gain_shard.reshape(channels, ND, 2, owned)
    gain_re = gain_pair[:, :, 0]
    gain_im = gain_pair[:, :, 1]
    new_re = (sum_re + gain_re * power) / (power + 1.0)
    new_im = (sum_im + gain_im * power) / (power + 1.0)
    averaged = jnp.stack([(gain_re + new_re) * 0.5, (gain_im + new_im) * 0.5], axis=2).reshape(
        channels, 2 * ND, owned
    )
    padded = extended(averaged, (("ch", 0),), 1)
    total_channels = channels * lax.axis_size("ch")
    chan_index = lax.axis_index("ch") * channels + jnp.arange(channels, dtype=jnp.int32)
    has_left = (chan_index > 0).astype(jnp.float32)[:, None, None]
    has_right = (chan_index < total_channels - 1).astype(jnp.float32)[:, None, None]
    return (0.25 * has_left * padded[:-2] + 0.5 * padded[1:-1] + 0.25 * has_right * padded[2:]) / (
        0.5 + 0.25 * has_left + 0.25 * has_right
    )


def body(facet_grid, kernel, tile_of, observed, flags, pairs, solver_order):
    channels = observed.shape[0]
    row_count = observed.shape[2]
    cell_count = kernel.shape[1]
    tile_count = facet_grid.shape[0]
    block_count = tile_of.shape[0]
    block_rows = row_count // block_count
    tile_pick = (tile_of[:, None] == jnp.arange(tile_count, dtype=jnp.int32)[None, :]).astype(
        jnp.bfloat16
    )
    kernel_blocks = kernel.reshape(block_count, block_rows, cell_count)
    chosen = jnp.einsum(
        "bt,tckg->bckg", tile_pick, facet_grid, preferred_element_type=jnp.float32
    ).astype(jnp.bfloat16)
    partial_vis = jnp.einsum(
        "bckg,bvg->ckbv", chosen, kernel_blocks, preferred_element_type=jnp.float32
    )
    summed = lax.psum_scatter(
        partial_vis.reshape(channels * lax.axis_size("ch"), partial_vis.shape[1], row_count).astype(
            jnp.bfloat16
        ),
        "ch",
        scatter_dimension=0,
        tiled=True,
    ).astype(jnp.float32)
    kept_rows = (1 - flags).astype(jnp.float32)
    model_vis = (summed * kept_rows[:, None, :]).astype(jnp.bfloat16)
    visible = (observed.astype(jnp.float32) * kept_rows[:, None, :]).astype(jnp.bfloat16)
    inverse = jnp.zeros((S,), jnp.int32).at[solver_order].set(jnp.arange(S, dtype=jnp.int32))
    bl_count = lax.axis_size("bl")
    owned = S // bl_count
    station_ids = jnp.arange(S, dtype=jnp.int32)[:, None]
    packed = pairs.reshape(1, 2, row_count)
    model_vis, visible, packed = (
        lax.all_to_all(model_vis, "bl", split_axis=2, concat_axis=2, tiled=True),
        lax.all_to_all(visible, "bl", split_axis=2, concat_axis=2, tiled=True),
        lax.all_to_all(packed, "bl", split_axis=2, concat_axis=2, tiled=True),
    )
    first_slot = inverse[packed[0, 0]]
    second_slot = inverse[packed[0, 1]]
    owner_slot = first_slot - lax.axis_index("bl") * owned
    near_pick = (owner_slot[None, :] == jnp.arange(owned, dtype=jnp.int32)[:, None]).astype(
        jnp.float32
    )
    far_pick = (second_slot[None, :] == station_ids).astype(jnp.float32)
    gain_shard = (
        jnp.zeros((channels, ND, 2, owned), jnp.float32)
        .at[:, :, 0, :]
        .set(1.0)
        .reshape(channels, 2 * ND, owned)
    )
    all_gains = (
        jnp.zeros((channels, ND, 2, S), jnp.float32)
        .at[:, :, 0, :]
        .set(1.0)
        .reshape(channels, 2 * ND, S)
    )
    for iteration in range(ITERS):
        if iteration > 0:
            all_gains = lax.all_gather(gain_shard, "bl", axis=2, tiled=True)
        far_gain = lookup(all_gains.reshape(channels * 2 * ND, S), far_pick)
        near_gain = lookup(gain_shard.reshape(channels * 2 * ND, owned), near_pick)
        stacked = row_terms(model_vis, visible, far_gain, near_gain)
        station_terms = jnp.einsum(
            "fv,sv->fs",
            stacked,
            near_pick,
            precision=lax.Precision.HIGHEST,
            preferred_element_type=jnp.float32,
        )
        mine = station_terms.reshape(channels, 3 * ND, owned)
        sum_re = mine[:, :ND]
        sum_im = mine[:, ND : 2 * ND]
        sum_power = mine[:, 2 * ND :]
        gain_shard = update_gains(gain_shard, sum_re, sum_im, sum_power)
    return gain_shard


def solution(mesh):
    in_specs = (
        P(None, None, None, "ch"),
        P("bl", "ch"),
        P("bl"),
        P("ch", None, "bl"),
        P("ch", "bl"),
        P(None, "bl"),
        P(),
    )
    out_specs = P("ch", None, "bl")
    return jax.shard_map(body, mesh=mesh, in_specs=in_specs, out_specs=out_specs, check_vma=False)
```

profile of v0, /device:TPU:1, one launch (start us, length us, event | category | flops | bytes accessed | tf_op | source)
XLA Modules:
  0.0 517.9 jit_solution(18245494994774000052)
XLA Ops:
  16.5 13.1 %all-to-all-start.1 = ((s32[1,2,2048]{1,0,2:T(1,128)}), s32[1,2,2048]{1,0,2:T(1,128)S(1)}, u32[]{:S(2)}, u32[]{:S(2)}) async-start(s32[1,2,2048]{1,0,2:T(1,128)} %bitcast.7), calls=%async_computation.2 | async-start | bytes 2097152 | tf_op jit(solution)/shard_map/all_to_all | solution.py:112
  35.0 23.2 %all-to-all-done.1 = s32[1,2,2048]{1,0,2:T(1,128)S(1)} async-done(((s32[1,2,2048]{1,0,2:T(1,128)}), s32[1,2,2048]{1,0,2:T(1,128)S(1)}, u32[]{:S(2)}, u32[]{:S(2)}) %all-to-all-start.1) | async-done | bytes 16416 | tf_op jit(solution)/shard_map/all_to_all | solution.py:112
  58.2 6.2 %all-to-all-start.2 = ((bf16[64,2,512]{2,1,0:T(2,128)(2,1)}), bf16[64,2,512]{2,1,0:T(2,128)(2,1)S(1)}, u32[]{:S(2)}, u32[]{:S(2)}) async-start(bf16[64,2,512]{2,1,0:T(2,128)(2,1)} %reshape.311), calls=%async_computation.3 | async-start | bytes 262144 | tf_op jit(solution)/shard_map/all_to_all | solution.py:111
  64.4 106.4 %slice_reduce_fusion = (s32[2048]{0:T(1024)S(1)}, s32[2048]{0:T(1024)S(1)}) fusion(s32[1,2,2048]{1,0,2:T(1,128)S(1)} %all-to-all-done.1), kind=kLoop, calls=%fused_computation.86 | loop fusion | bytes 32768 | tf_op jit(solution)/shard_map/slice | solution.py:114
  172.4 8.6 %copy.107 = bf16[16,16,2048]{1,0,2:T(8,128)(2,1)} copy(bf16[16,16,2048]{2,1,0:T(8,128)(2,1)S(1)} %multiply_convert_fusion) | data formatting | bytes 2097152 | tf_op jit(solution)/shard_map/convert_element_type | solution.py:102
  181.0 12.5 %reshape.309 = bf16[64,2,4096]{2,1,0:T(2,128)(2,1)} reshape(bf16[2048,16,16]{2,1,0:T(8,128)(2,1)} %bitcast.247) | data formatting | bytes 2097152
  193.4 10.7 %all-to-all-start = ((bf16[64,2,4096]{2,1,0:T(2,128)(2,1)}), bf16[64,2,4096]{2,1,0:T(2,128)(2,1)S(1)}, u32[]{:S(2)}, u32[]{:S(2)}) async-start(bf16[64,2,4096]{2,1,0:T(2,128)(2,1)} %reshape.309), calls=%async_computation.1 | async-start | bytes 2097152 | tf_op jit(solution)/shard_map/all_to_all | solution.py:110
  204.1 13.2 %gather_fusion.1 = s32[2048]{0:T(1024)S(1)} fusion(s32[512]{0:T(512)S(1)} %scatter_custom_fusion, s32[2048]{0:T(1024)S(1)} %broadcast_clamp_fusion), kind=kCustom, calls=%fused_computation.1 | custom fusion | bytes 24576 | tf_op jit(solution)/shard_map/gather | solution.py:114
  217.4 13.2 %gather_fusion = s32[2048]{0:T(1024)S(1)} fusion(s32[512]{0:T(512)S(1)} %scatter_custom_fusion, s32[2048]{0:T(1024)S(1)} %broadcast_clamp_fusion.1), kind=kCustom, calls=%fused_computation | custom fusion | bytes 24576 | tf_op jit(solution)/shard_map/gather | solution.py:115
  233.0 3.4 fusion.8
  242.2 7.6 %reshape.310 = bf16[2048,16,16]{2,1,0:T(8,128)(2,1)} reshape(bf16[64,2,4096]{2,1,0:T(2,128)(2,1)S(1)} %all-to-all-done) | data formatting | bytes 2097152
  249.8 9.1 %copy.108 = bf16[16,16,2048]{2,0,1:T(8,128)(2,1)S(1)} copy(bf16[16,16,2048]{1,0,2:T(8,128)(2,1)} %bitcast.248) | data formatting | bytes 2097152 | tf_op jit(solution)/shard_map/all_to_all | solution.py:110
  264.0 3.9 fusion.10
  269.7 4.0 collective-permute-start
  274.7 56.0 %all_gather.9 = f32[16,16,512]{0,2,1:T(8,128)} all-gather(f32[16,16,8]{0,2,1:T(8,128)S(1)} %fusion.111), channel_id=1, replica_groups=mesh['bl'=64,'ch'=4] {'bl'}, dimensions={2}, use_global_device_ids=true | all-gather | bytes 532480 | tf_op jit(solution)/shard_map/all_gather | solution.py:135
  342.3 3.9 fusion.16
  346.7 3.6 collective-permute-start.2
  352.0 3.6 collective-permute-done.3
  355.7 53.5 %all_gather.10 = f32[16,16,512]{0,2,1:T(8,128)} all-gather(f32[16,16,8]{0,2,1:T(8,128)S(1)} %fusion.98), channel_id=1, replica_groups=mesh['bl'=64,'ch'=4] {'bl'}, dimensions={2}, use_global_device_ids=true | all-gather | bytes 532480 | tf_op jit(solution)/shard_map/all_gather | solution.py:135
  420.8 3.9 fusion.22
  430.0 3.6 collective-permute-done.5
  433.6 53.5 %all_gather.11 = f32[16,16,512]{0,2,1:T(8,128)} all-gather(f32[16,16,8]{0,2,1:T(8,128)S(1)} %fusion.85), channel_id=1, replica_groups=mesh['bl'=64,'ch'=4] {'bl'}, dimensions={2}, use_global_device_ids=true | all-gather | bytes 532480 | tf_op jit(solution)/shard_map/all_gather | solution.py:135
  497.2 3.9 fusion.28
  506.4 3.6 collective-permute-done.7
  (156 shorter events, 79.0 us)
Async XLA Ops:
  6.5 4.0 copy-start.3
  6.5 164.3 %reduce-scatter.2.cloned.1.call-start = ((), (), s32[]{:S(2)}) async-start(), calls=%async_computation.4 | async-start | bytes 5242880 | tf_op jit(solution)/shard_map/reduce_scatter | solution.py:93
  14.5 15.2 %copy-start.19 = (s32[512]{0:T(512)S(1)}, s32[512]{0:T(512)}, u32[]{:S(2)}) copy-start(s32[512]{0:T(512)} %param.17) | copy-start | bytes 6148
  14.5 15.3 %copy-start.10 = (s32[16,2048]{1,0:T(8,128)S(1)}, s32[16,2048]{1,0:T(8,128)}, u32[]{:S(2)}) copy-start(s32[16,2048]{1,0:T(8,128)} %param.15) | copy-start | bytes 393220
  14.5 15.3 %copy-start.8 = (bf16[16,2,2048]{2,1,0:T(2,128)(2,1)S(1)}, bf16[16,2,2048]{2,1,0:T(2,128)(2,1)}, u32[]{:S(2)}) copy-start(bf16[16,2,2048]{2,1,0:T(2,128)(2,1)} %param.14) | copy-start | bytes 393220
  16.5 41.7 %all-to-all-start.1 = ((s32[1,2,2048]{1,0,2:T(1,128)}), s32[1,2,2048]{1,0,2:T(1,128)S(1)}, u32[]{:S(2)}, u32[]{:S(2)}) async-start(s32[1,2,2048]{1,0,2:T(1,128)} %bitcast.7), calls=%async_computation.2 | async-start | bytes 2097152 | tf_op jit(solution)/shard_map/all_to_all | solution.py:112
  29.9 244.7 %copy-start.12 = (f32[16]{0:T(128)}, f32[16]{0:T(128)S(1)}, u32[]{:S(2)}) copy-start(f32[16]{0:T(128)S(1)} %add_add_fusion) | copy-start | bytes 196
  58.2 135.2 %all-to-all-start.2 = ((bf16[64,2,512]{2,1,0:T(2,128)(2,1)}), bf16[64,2,512]{2,1,0:T(2,128)(2,1)S(1)}, u32[]{:S(2)}, u32[]{:S(2)}) async-start(bf16[64,2,512]{2,1,0:T(2,128)(2,1)} %reshape.311), calls=%async_computation.3 | async-start | bytes 262144 | tf_op jit(solution)/shard_map/all_to_all | solution.py:111
  193.4 48.7 %all-to-all-start = ((bf16[64,2,4096]{2,1,0:T(2,128)(2,1)}), bf16[64,2,4096]{2,1,0:T(2,128)(2,1)S(1)}, u32[]{:S(2)}, u32[]{:S(2)}) async-start(bf16[64,2,4096]{2,1,0:T(2,128)(2,1)} %reshape.309), calls=%async_computation.1 | async-start | bytes 2097152 | tf_op jit(solution)/shard_map/all_to_all | solution.py:110
  217.4 13.3 %copy-start.9 = (f32[16,8,2,8]{3,1,0,2:T(8,128)S(1)}, f32[16,8,2,8]{3,1,0,2:T(8,128)}, u32[]{:S(2)}) copy-start(f32[16,8,2,8]{3,1,0,2:T(8,128)} %constant.98) | copy-start | bytes 24580
  217.4 15.6 %copy-start.20 = (f32[16,8,2,512]{3,1,2,0:T(8,128)S(1)}, f32[16,8,2,512]{3,1,2,0:T(8,128)}, u32[]{:S(2)}) copy-start(f32[16,8,2,512]{3,1,2,0:T(8,128)} %constant.89.clone.1) | copy-start | bytes 1572868
  230.6 103.8 %copy-start.16 = (s32[2048]{0:T(1024)}, s32[2048]{0:T(1024)S(1)}, u32[]{:S(2)}) copy-start(s32[2048]{0:T(1024)S(1)} %gather_fusion) | copy-start | bytes 24580
  268.3 6.3 %collective-permute-start.1 = (f32[1,16,8]{0,2,1:T(8,128)S(1)}, f32[1,16,8]{0,2,1:T(8,128)S(1)}, u32[]{:S(2)}, u32[]{:S(2)}) collective-permute-start(f32[1,16,8]{0,2,1:T(8,128)S(1)} %copy.127), channel_id=1, source_target_pairs={{1,0},{2,1},{3,2},{5,4},{6,5},{7,6},{9,8},{10,9},{11,10},{13,12},{... | collective-permute-start | bytes 1544 | tf_op jit(solution)/shard_map/ppermute | solution.py:19
  269.7 4.8 collective-permute-start
  342.3 13.2 %copy-start.13 = (f32[16]{0:T(128)S(1)}, f32[16]{0:T(128)}, u32[]{:S(2)}) copy-start(f32[16]{0:T(128)} %copy-done.12) | copy-start | bytes 196
  346.7 5.3 %collective-permute-start.2 = (f32[1,16,8]{0,2,1:T(8,128)S(1)}, f32[1,16,8]{0,2,1:T(8,128)S(1)}, u32[]{:S(2)}, u32[]{:S(2)}) collective-permute-start(f32[1,16,8]{0,2,1:T(8,128)S(1)} %copy.138), channel_id=1, source_target_pairs={{0,1},{1,2},{2,3},{4,5},{5,6},{6,7},{8,9},{9,10},{10,11},{12,13},{... | collective-permute-start | bytes 1544 | tf_op jit(solution)/shard_map/ppermute | solution.py:18
  350.6 5.0 collective-permute-start.3
  420.8 12.7 %copy-start.14 = (f32[16]{0:T(128)S(1)}, f32[16]{0:T(128)}, u32[]{:S(2)}) copy-start(f32[16]{0:T(128)} %copy-done.12) | copy-start | bytes 196
  425.1 4.8 collective-permute-start.4
  428.5 5.0 collective-permute-start.5
  495.4 15.4 %copy-start.1 = (bf16[4,64,16,256]{3,2,1,0:T(8,128)(2,1)S(1)}, bf16[4,64,16,256]{3,2,1,0:T(8,128)(2,1)}, u32[]{:S(2)}) copy-start(bf16[4,64,16,256]{3,2,1,0:T(8,128)(2,1)} %param.11) | copy-start | bytes 6291460
  497.2 12.7 %copy-start.15 = (f32[16]{0:T(128)S(1)}, f32[16]{0:T(128)}, u32[]{:S(2)}) copy-start(f32[16]{0:T(128)} %copy-done.12) | copy-start | bytes 196
  501.6 4.8 collective-permute-start.6
  504.9 5.0 collective-permute-start.7
  (9 other events, 26.4 us)
Sparse Core Ops, SparseCore 0:
  14.6 53.0 reduce-scatter.1
where the time goes:
time: 525 us; the launch traced here: 518 us
  local copies, waits for them, and re-layouts  209 us (40%)
  blocking collectives  163 us (31%)
  starting transfers between devices  49 us (9%)
  waiting for transfers between devices  34.6 us (7%)
  matrix products  34.3 us (7%)
  between operations  14.5 us (3%)
  other arithmetic  13.8 us (3%)
    all_gather x3, blocking collectives, body(): all_gains = lax.all_gather(gain_shard, 'bl', axis=2, tiled=True)  163 us
    slice x1, local copies, waits for them, and re-layouts, body(): first_slot = inverse[packed[0, 0]]  106 us
    unnamed x55, local copies, waits for them, and re-layouts  36.5 us
    all_to_all x1, waiting for transfers between devices, body(): lax.all_to_all(packed, 'bl', split_axis=2, concat_axis=2, tiled=True)  23.2 us
    dot_general x4, matrix products, body(): jnp.einsum('fv,sv->fs', stacked, near_pick, precision=lax.Precision.HIGHE...  15.8 us
    dot_general x8, matrix products, lookup(): jnp.dot(gain_flat, pick, precision=lax.Precision.HIGHEST, preferred_eleme...  14.9 us
    ppermute x4, starting transfers between devices, extended(): before = lax.ppermute(last, axis, up)  13.8 us
    gather x1, local copies, waits for them, and re-layouts, body(): first_slot = inverse[packed[0, 0]]  13.2 us
  transfers between devices with their start and end apart: 12, of which 5 were waited for; matrix products, arithmetic and copies ran while one was open for 34% of the time, Pallas kernels for 0%

commit v1 on v0

--- a/solution.py
+++ b/solution.py
@@ -132,7 +132,9 @@
     )
     for iteration in range(ITERS):
         if iteration > 0:
-            all_gains = lax.all_gather(gain_shard, "bl", axis=2, tiled=True)
+            all_gains = jnp.concatenate(
+                lax.all_to_all(jnp.stack([gain_shard] * lax.axis_size("bl")), "bl", 0, 0), axis=2
+            )
         far_gain = lookup(all_gains.reshape(channels * 2 * ND, S), far_pick)
         near_gain = lookup(gain_shard.reshape(channels * 2 * ND, owned), near_pick)
         stacked = row_terms(model_vis, visible, far_gain, near_gain)

time: 525 us -> 487 us (0.928)
  blocking collectives: 163 us -> 0 us
  local copies, waits for them, and re-layouts: 209 us -> 254 us
  waiting for transfers between devices: 34.6 us -> 78.6 us
  starting transfers between devices: 49 us -> 76.2 us
    all_gather x3 -> x0, blocking collectives: 163 us -> none  [body(): all_gains = lax.all_gather(gain_shard, 'bl', axis=2, tiled=True)]
    all_to_all x0 -> x3, waiting for transfers between devices: none -> 43.9 us  [body(): lax.all_to_all(jnp.stack([gain_shard] * lax.axis_size('bl')), 'bl', 0, 0)]
    all_to_all x0 -> x3, starting transfers between devices: none -> 27.1 us  [body(): lax.all_to_all(jnp.stack([gain_shard] * lax.axis_size('bl')), 'bl', 0, 0)]
    unnamed x55 -> x48, local copies, waits for them, and re-layouts: 36.5 us -> 59.8 us
    reshape x0 -> x6, local copies, waits for them, and re-layouts: none -> 14.5 us  [body(): jnp.concatenate(lax.all_to_all(jnp.stack([gain_shard] * lax.axis_size('bl...]
    slice x1, local copies, waits for them, and re-layouts: 106 us -> 115 us  [body(): first_slot = inverse[packed[0, 0]]]
    all_to_all x0 -> x3, other arithmetic: none -> 5.65 us  [body(): lax.all_to_all(jnp.stack([gain_shard] * lax.axis_size('bl')), 'bl', 0, 0)]
  transfers between devices with their start and end apart: 12 -> 15, of which waited for: 5 -> 8; matrix products, arithmetic and copies ran while one was open for 34% -> 40% of each run, Pallas kernels for 0% -> 0%
where the time goes in v1:
time: 487 us; the launch traced here: 480 us
  local copies, waits for them, and re-layouts  254 us (52%)
  waiting for transfers between devices  78.6 us (16%)
  starting transfers between devices  76.2 us (16%)
  matrix products  38.4 us (8%)
  other arithmetic  17.7 us (4%)
  between operations  14.5 us (3%)
    slice x1, local copies, waits for them, and re-layouts, body(): first_slot = inverse[packed[0, 0]]  115 us
    unnamed x48, local copies, waits for them, and re-layouts  59.8 us
    all_to_all x3, waiting for transfers between devices, body(): lax.all_to_all(jnp.stack([gain_shard] * lax.axis_size('bl')), 'bl', 0, 0)  43.9 us
    all_to_all x3, starting transfers between devices, body(): lax.all_to_all(jnp.stack([gain_shard] * lax.axis_size('bl')), 'bl', 0, 0)  27.1 us
    all_to_all x1, waiting for transfers between devices, body(): lax.all_to_all(packed, 'bl', split_axis=2, concat_axis=2, tiled=True)  23.3 us
    dot_general x8, matrix products, lookup(): jnp.dot(gain_flat, pick, precision=lax.Precision.HIGHEST, preferred_eleme...  18.9 us
    dot_general x4, matrix products, body(): jnp.einsum('fv,sv->fs', stacked, near_pick, precision=lax.Precision.HIGHE...  15.8 us
    reshape x6, local copies, waits for them, and re-layouts, body(): jnp.concatenate(lax.all_to_all(jnp.stack([gain_shard] * lax.axis_size('bl...  14.5 us
  transfers between devices with their start and end apart: 15, of which 8 were waited for; matrix products, arithmetic and copies ran while one was open for 40% of the time, Pallas kernels for 0%

profile of v1, /device:TPU:1, one launch (start us, length us, event | category | flops | bytes accessed | tf_op | source)
XLA Modules:
  0.0 479.7 jit_solution(3743086793518295845)
XLA Ops:
  16.6 13.1 %all-to-all-start.1 = ((s32[1,2,2048]{1,0,2:T(1,128)}), s32[1,2,2048]{1,0,2:T(1,128)S(1)}, u32[]{:S(2)}, u32[]{:S(2)}) async-start(s32[1,2,2048]{1,0,2:T(1,128)} %bitcast.7), calls=%async_computation.2 | async-start | bytes 2097152 | tf_op jit(solution)/shard_map/all_to_all | solution.py:112
  35.0 23.3 %all-to-all-done.1 = s32[1,2,2048]{1,0,2:T(1,128)S(1)} async-done(((s32[1,2,2048]{1,0,2:T(1,128)}), s32[1,2,2048]{1,0,2:T(1,128)S(1)}, u32[]{:S(2)}, u32[]{:S(2)}) %all-to-all-start.1) | async-done | bytes 16416 | tf_op jit(solution)/shard_map/all_to_all | solution.py:112
  58.3 6.2 %all-to-all-start.2 = ((bf16[64,2,512]{2,1,0:T(2,128)(2,1)}), bf16[64,2,512]{2,1,0:T(2,128)(2,1)S(1)}, u32[]{:S(2)}, u32[]{:S(2)}) async-start(bf16[64,2,512]{2,1,0:T(2,128)(2,1)} %reshape.326), calls=%async_computation.3 | async-start | bytes 262144 | tf_op jit(solution)/shard_map/all_to_all | solution.py:111
  64.5 115.0 %slice_reduce_fusion = (s32[2048]{0:T(1024)S(1)}, s32[2048]{0:T(1024)S(1)}) fusion(s32[1,2,2048]{1,0,2:T(1,128)S(1)} %all-to-all-done.1), kind=kLoop, calls=%fused_computation.86 | loop fusion | bytes 32768 | tf_op jit(solution)/shard_map/slice | solution.py:114
  181.1 8.6 %copy.107 = bf16[16,16,2048]{1,0,2:T(8,128)(2,1)} copy(bf16[16,16,2048]{2,1,0:T(8,128)(2,1)S(1)} %multiply_convert_fusion) | data formatting | bytes 2097152 | tf_op jit(solution)/shard_map/convert_element_type | solution.py:102
  189.6 12.5 %reshape.324 = bf16[64,2,4096]{2,1,0:T(2,128)(2,1)} reshape(bf16[2048,16,16]{2,1,0:T(8,128)(2,1)} %bitcast.265) | data formatting | bytes 2097152
  202.1 10.6 %all-to-all-start = ((bf16[64,2,4096]{2,1,0:T(2,128)(2,1)}), bf16[64,2,4096]{2,1,0:T(2,128)(2,1)S(1)}, u32[]{:S(2)}, u32[]{:S(2)}) async-start(bf16[64,2,4096]{2,1,0:T(2,128)(2,1)} %reshape.324), calls=%async_computation.1 | async-start | bytes 2097152 | tf_op jit(solution)/shard_map/all_to_all | solution.py:110
  212.7 13.2 %gather_fusion.1 = s32[2048]{0:T(1024)S(1)} fusion(s32[512]{0:T(512)S(1)} %scatter_custom_fusion, s32[2048]{0:T(1024)S(1)} %broadcast_clamp_fusion), kind=kCustom, calls=%fused_computation.1 | custom fusion | bytes 24576 | tf_op jit(solution)/shard_map/gather | solution.py:114
  226.0 13.2 %gather_fusion = s32[2048]{0:T(1024)S(1)} fusion(s32[512]{0:T(512)S(1)} %scatter_custom_fusion, s32[2048]{0:T(1024)S(1)} %broadcast_clamp_fusion.1), kind=kCustom, calls=%fused_computation | custom fusion | bytes 24576 | tf_op jit(solution)/shard_map/gather | solution.py:115
  250.7 7.6 %reshape.325 = bf16[2048,16,16]{2,1,0:T(8,128)(2,1)} reshape(bf16[64,2,4096]{2,1,0:T(2,128)(2,1)S(1)} %all-to-all-done) | data formatting | bytes 2097152
  258.3 9.1 %copy.108 = bf16[16,16,2048]{2,0,1:T(8,128)(2,1)S(1)} copy(bf16[16,16,2048]{1,0,2:T(8,128)(2,1)} %bitcast.266) | data formatting | bytes 2097152 | tf_op jit(solution)/shard_map/all_to_all | solution.py:110
  272.5 3.9 fusion.10
  278.2 4.0 collective-permute-start
  285.7 4.6 reshape.328
  290.3 11.5 %all-to-all-start.3 = ((f32[64,1,2048]{2,1,0:T(1,128)}), f32[64,1,2048]{2,1,0:T(1,128)S(1)}, u32[]{:S(2)}, u32[]{:S(2)}) async-start(f32[64,1,2048]{2,1,0:T(1,128)} %reshape.328), calls=%async_computation.4 | async-start | bytes 1048576 | tf_op jit(solution)/shard_map/all_to_all | solution.py:136
  304.4 14.6 %all-to-all-done.3 = f32[64,1,2048]{2,1,0:T(1,128)S(1)} async-done(((f32[64,1,2048]{2,1,0:T(1,128)}), f32[64,1,2048]{2,1,0:T(1,128)S(1)}, u32[]{:S(2)}, u32[]{:S(2)}) %all-to-all-start.3) | async-done | bytes 524320 | tf_op jit(solution)/shard_map/all_to_all | solution.py:136
  336.0 3.9 fusion.16
  352.2 4.2 reshape.330
  356.4 8.0 %all-to-all-start.4 = ((f32[64,1,2048]{2,1,0:T(1,128)}), f32[64,1,2048]{2,1,0:T(1,128)S(1)}, u32[]{:S(2)}, u32[]{:S(2)}) async-start(f32[64,1,2048]{2,1,0:T(1,128)} %reshape.330), calls=%async_computation.5 | async-start | bytes 1048576 | tf_op jit(solution)/shard_map/all_to_all | solution.py:136
  367.0 14.6 %all-to-all-done.4 = f32[64,1,2048]{2,1,0:T(1,128)S(1)} async-done(((f32[64,1,2048]{2,1,0:T(1,128)}), f32[64,1,2048]{2,1,0:T(1,128)S(1)}, u32[]{:S(2)}, u32[]{:S(2)}) %all-to-all-start.4) | async-done | bytes 524320 | tf_op jit(solution)/shard_map/all_to_all | solution.py:136
  413.4 4.2 reshape.332
  417.6 7.6 %all-to-all-start.5 = ((f32[64,1,2048]{2,1,0:T(1,128)}), f32[64,1,2048]{2,1,0:T(1,128)S(1)}, u32[]{:S(2)}, u32[]{:S(2)}) async-start(f32[64,1,2048]{2,1,0:T(1,128)} %reshape.332), calls=%async_computation.6 | async-start | bytes 1048576 | tf_op jit(solution)/shard_map/all_to_all | solution.py:136
  427.9 14.6 %all-to-all-done.5 = f32[64,1,2048]{2,1,0:T(1,128)S(1)} async-done(((f32[64,1,2048]{2,1,0:T(1,128)}), f32[64,1,2048]{2,1,0:T(1,128)S(1)}, u32[]{:S(2)}, u32[]{:S(2)}) %all-to-all-start.5) | async-done | bytes 524320 | tf_op jit(solution)/shard_map/all_to_all | solution.py:136
  459.0 3.9 fusion.28
  (162 shorter events, 133.0 us)
Async XLA Ops:
  6.5 4.0 copy-start.6
  6.5 173.0 %reduce-scatter.2.cloned.1.call-start = ((), (), s32[]{:S(2)}) async-start(), calls=%async_computation.7 | async-start | bytes 5242880 | tf_op jit(solution)/shard_map/reduce_scatter | solution.py:93
  14.5 15.3 %copy-start.11 = (s32[512]{0:T(512)S(1)}, s32[512]{0:T(512)}, u32[]{:S(2)}) copy-start(s32[512]{0:T(512)} %param.17) | copy-start | bytes 6148
  14.5 15.3 %copy-start.9 = (s32[16,2048]{1,0:T(8,128)S(1)}, s32[16,2048]{1,0:T(8,128)}, u32[]{:S(2)}) copy-start(s32[16,2048]{1,0:T(8,128)} %param.15) | copy-start | bytes 393220
  14.5 15.3 %copy-start.7 = (bf16[16,2,2048]{2,1,0:T(2,128)(2,1)S(1)}, bf16[16,2,2048]{2,1,0:T(2,128)(2,1)}, u32[]{:S(2)}) copy-start(bf16[16,2,2048]{2,1,0:T(2,128)(2,1)} %param.14) | copy-start | bytes 393220
  16.6 41.7 %all-to-all-start.1 = ((s32[1,2,2048]{1,0,2:T(1,128)}), s32[1,2,2048]{1,0,2:T(1,128)S(1)}, u32[]{:S(2)}, u32[]{:S(2)}) async-start(s32[1,2,2048]{1,0,2:T(1,128)} %bitcast.7), calls=%async_computation.2 | async-start | bytes 2097152 | tf_op jit(solution)/shard_map/all_to_all | solution.py:112
  58.3 143.8 %all-to-all-start.2 = ((bf16[64,2,512]{2,1,0:T(2,128)(2,1)}), bf16[64,2,512]{2,1,0:T(2,128)(2,1)S(1)}, u32[]{:S(2)}, u32[]{:S(2)}) async-start(bf16[64,2,512]{2,1,0:T(2,128)(2,1)} %reshape.326), calls=%async_computation.3 | async-start | bytes 262144 | tf_op jit(solution)/shard_map/all_to_all | solution.py:111
  202.1 48.6 %all-to-all-start = ((bf16[64,2,4096]{2,1,0:T(2,128)(2,1)}), bf16[64,2,4096]{2,1,0:T(2,128)(2,1)S(1)}, u32[]{:S(2)}, u32[]{:S(2)}) async-start(bf16[64,2,4096]{2,1,0:T(2,128)(2,1)} %reshape.324), calls=%async_computation.1 | async-start | bytes 2097152 | tf_op jit(solution)/shard_map/all_to_all | solution.py:110
  226.0 13.3 %copy-start.8 = (f32[16,8,2,8]{3,1,0,2:T(8,128)S(1)}, f32[16,8,2,8]{3,1,0,2:T(8,128)}, u32[]{:S(2)}) copy-start(f32[16,8,2,8]{3,1,0,2:T(8,128)} %constant.98) | copy-start | bytes 24580
  226.0 15.6 %copy-start.12 = (f32[16,8,2,512]{3,1,2,0:T(8,128)S(1)}, f32[16,8,2,512]{3,1,2,0:T(8,128)}, u32[]{:S(2)}) copy-start(f32[16,8,2,512]{3,1,2,0:T(8,128)} %constant.89.clone.1) | copy-start | bytes 1572868
  276.8 6.3 %collective-permute-start.1 = (f32[1,16,8]{0,2,1:T(8,128)S(1)}, f32[1,16,8]{0,2,1:T(8,128)S(1)}, u32[]{:S(2)}, u32[]{:S(2)}) collective-permute-start(f32[1,16,8]{0,2,1:T(8,128)S(1)} %copy.127), channel_id=1, source_target_pairs={{1,0},{2,1},{3,2},{5,4},{6,5},{7,6},{9,8},{10,9},{11,10},{13,12},{... | collective-permute-start | bytes 1544 | tf_op jit(solution)/shard_map/ppermute | solution.py:19
  278.2 4.8 collective-permute-start
  290.3 28.8 %all-to-all-start.3 = ((f32[64,1,2048]{2,1,0:T(1,128)}), f32[64,1,2048]{2,1,0:T(1,128)S(1)}, u32[]{:S(2)}, u32[]{:S(2)}) async-start(f32[64,1,2048]{2,1,0:T(1,128)} %reshape.328), calls=%async_computation.4 | async-start | bytes 1048576 | tf_op jit(solution)/shard_map/all_to_all | solution.py:136
  332.0 2.1 copy-start.4
  340.4 5.6 %collective-permute-start.2 = (f32[1,16,8]{0,2,1:T(8,128)S(1)}, f32[1,16,8]{0,2,1:T(8,128)S(1)}, u32[]{:S(2)}, u32[]{:S(2)}) collective-permute-start(f32[1,16,8]{0,2,1:T(8,128)S(1)} %copy.138), channel_id=1, source_target_pairs={{0,1},{1,2},{2,3},{4,5},{5,6},{6,7},{8,9},{9,10},{10,11},{12,13},{... | collective-permute-start | bytes 1544 | tf_op jit(solution)/shard_map/ppermute | solution.py:18
  344.6 5.0 %collective-permute-start.3 = (f32[1,16,8]{0,2,1:T(8,128)S(1)}, f32[1,16,8]{0,2,1:T(8,128)S(1)}, u32[]{:S(2)}, u32[]{:S(2)}) collective-permute-start(f32[1,16,8]{0,2,1:T(8,128)S(1)} %copy.141), channel_id=1, source_target_pairs={{1,0},{2,1},{3,2},{5,4},{6,5},{7,6},{9,8},{10,9},{11,10},{13,12},{... | collective-permute-start | bytes 1544 | tf_op jit(solution)/shard_map/ppermute | solution.py:19
  356.4 25.3 %all-to-all-start.4 = ((f32[64,1,2048]{2,1,0:T(1,128)}), f32[64,1,2048]{2,1,0:T(1,128)S(1)}, u32[]{:S(2)}, u32[]{:S(2)}) async-start(f32[64,1,2048]{2,1,0:T(1,128)} %reshape.330), calls=%async_computation.5 | async-start | bytes 1048576 | tf_op jit(solution)/shard_map/all_to_all | solution.py:136
  402.4 4.8 collective-permute-start.4
  405.8 5.0 %collective-permute-start.5 = (f32[1,16,8]{0,2,1:T(8,128)S(1)}, f32[1,16,8]{0,2,1:T(8,128)S(1)}, u32[]{:S(2)}, u32[]{:S(2)}) collective-permute-start(f32[1,16,8]{0,2,1:T(8,128)S(1)} %copy.155), channel_id=1, source_target_pairs={{1,0},{2,1},{3,2},{5,4},{6,5},{7,6},{9,8},{10,9},{11,10},{13,12},{... | collective-permute-start | bytes 1544 | tf_op jit(solution)/shard_map/ppermute | solution.py:19
  417.6 24.9 %all-to-all-start.5 = ((f32[64,1,2048]{2,1,0:T(1,128)}), f32[64,1,2048]{2,1,0:T(1,128)S(1)}, u32[]{:S(2)}, u32[]{:S(2)}) async-start(f32[64,1,2048]{2,1,0:T(1,128)} %reshape.332), calls=%async_computation.6 | async-start | bytes 1048576 | tf_op jit(solution)/shard_map/all_to_all | solution.py:136
  454.9 2.1 copy-start.3
  458.5 14.1 %copy-start.1 = (bf16[4,64,16,256]{3,2,1,0:T(8,128)(2,1)S(1)}, bf16[4,64,16,256]{3,2,1,0:T(8,128)(2,1)}, u32[]{:S(2)}) copy-start(bf16[4,64,16,256]{3,2,1,0:T(8,128)(2,1)} %param.11) | copy-start | bytes 6291460
  463.4 4.8 %collective-permute-start.6 = (f32[1,16,8]{0,2,1:T(8,128)S(1)}, f32[1,16,8]{0,2,1:T(8,128)S(1)}, u32[]{:S(2)}, u32[]{:S(2)}) collective-permute-start(f32[1,16,8]{0,2,1:T(8,128)S(1)} %copy.166), channel_id=1, source_target_pairs={{0,1},{1,2},{2,3},{4,5},{5,6},{6,7},{8,9},{9,10},{10,11},{12,13},{... | collective-permute-start | bytes 1544 | tf_op jit(solution)/shard_map/ppermute | solution.py:18
  466.7 5.0 %collective-permute-start.7 = (f32[1,16,8]{0,2,1:T(8,128)S(1)}, f32[1,16,8]{0,2,1:T(8,128)S(1)}, u32[]{:S(2)}, u32[]{:S(2)}) collective-permute-start(f32[1,16,8]{0,2,1:T(8,128)S(1)} %copy.169), channel_id=1, source_target_pairs={{1,0},{2,1},{3,2},{5,4},{6,5},{7,6},{9,8},{10,9},{11,10},{13,12},{... | collective-permute-start | bytes 1544 | tf_op jit(solution)/shard_map/ppermute | solution.py:19
  (4 other events, 6.0 us)
Sparse Core Ops, SparseCore 0:
  14.6 53.0 reduce-scatter.1
